TPU v7x, 32 devices: a whole 2x2x4 slice. The times are simulated.
32 devices in a mesh: seq: 16 (over z, x, core), ex: 2 (over y).
Axes of the slice: x: 2, y: 2, z: 4, core: 2. Of those that a mesh axis runs over, the one named last changes fastest.
Arguments:
- acts: bfloat16 [4, 2048, 4096], P('ex', 'seq'), may hold values from -6 to 6
- out_grads: bfloat16 [4, 2048, 5120], P('ex', 'seq'), may hold values from -6 to 6
- lengths: int32 [4], P('ex'), may hold values from 512 to 2048, as said below
- in_tiles: bfloat16 [32, 128, 128], replicated, may hold values from -0.09375 to 0.09375
- in_blocks: int32 [32], replicated, may hold values from 0 to 31, each once
- in_signs: int32 [32, 128], replicated, may hold values 0 or 1
- out_tiles: bfloat16 [40, 128, 64], replicated, may hold values from -0.09375 to 0.09375
- out_blocks: int32 [40], replicated, may hold values from 0 to 39, as said below
- out_signs: int32 [40, 128], replicated, may hold values 0 or 1
- query_grads: bfloat16 [2048, 8192], P('seq', 'ex'), may hold values from -6 to 6
Outputs:
- scores: float32 [4, 2048], P('ex', 'seq')
Inputs may be any that keep to these rules, and one draw needn't show every extreme that they name: `lengths`: every training sequence has at least 512 live positions and some sequence has all 2048. `in_blocks`: a permutation of the 32 input feature blocks. `out_blocks`: the first 32 entries are a permutation of 0 to 31, the last 8 a permutation of 32 to 39.
All inputs are finite; a program needn't handle non-finite values.
Results may differ from a plain program's by a relative error of at most 0.005.
Values may be sent and summed in bfloat16 or wider, within the bound.
A program may use at most 64 MiB of HBM per device.

v0:
```python
import jax
import jax.numpy as jnp
from jax import lax
from jax.sharding import PartitionSpec as P


def place(sketch_tiles, block_ids, sign_bits):
    tile_count = sketch_tiles.shape[0]
    chosen = (block_ids[:, None] == jnp.arange(tile_count, dtype=jnp.int32)[None, :]).astype(
        jnp.float32
    )
    signed = sketch_tiles.astype(jnp.float32) * (2 * sign_bits - 1).astype(jnp.float32)[:, :, None]
    placed = jnp.einsum("bc,bik->cik", chosen, signed, precision=lax.Precision.HIGHEST)
    return placed.reshape(tile_count * sketch_tiles.shape[1], sketch_tiles.shape[2]).astype(
        jnp.bfloat16
    )


def widen(placed, split_at):
    out_cols = placed.shape[1]
    upper = jnp.concatenate([placed[:split_at], jnp.zeros((split_at, out_cols), jnp.bfloat16)], 1)
    lower = jnp.concatenate(
        [jnp.zeros((placed.shape[0] - split_at, out_cols), jnp.bfloat16), placed[split_at:]], 1
    )
    return jnp.concatenate([upper, lower], 0)


def per_device(
    acts,
    out_grads,
    lengths,
    in_tiles,
    in_blocks,
    in_signs,
    out_tiles,
    out_blocks,
    out_signs,
    query_grads,
):
    examples_dev, seq_dev, width = acts.shape
    r_in = place(in_tiles, in_blocks, in_signs)
    r_out = widen(place(out_tiles, out_blocks, out_signs), width)
    offset = lax.axis_index("seq") * seq_dev
    positions = offset + jnp.arange(seq_dev, dtype=jnp.int32)
    live_rows = (positions[None, :] < lengths[:, None]).astype(jnp.float32)
    in_sketched = jnp.dot(
        acts.reshape(examples_dev * seq_dev, width), r_in, preferred_element_type=jnp.float32
    )
    in_sketched = (in_sketched.reshape(examples_dev, seq_dev, -1) * live_rows[:, :, None]).astype(
        jnp.bfloat16
    )
    out_sketched = jnp.dot(
        out_grads.reshape(examples_dev * seq_dev, -1), r_out, preferred_element_type=jnp.float32
    )
    out_sketched = out_sketched.reshape(examples_dev, seq_dev, -1).astype(jnp.bfloat16)
    crossed = jnp.einsum(
        "esa,esc->eac", in_sketched, out_sketched, preferred_element_type=jnp.float32
    )
    in_cols = r_in.shape[1] // 2
    out_cols = r_out.shape[1] // 2
    partial_proj = jnp.stack([crossed[:, :in_cols, :out_cols], crossed[:, in_cols:, out_cols:]], 1)
    partial_proj = partial_proj.reshape(examples_dev, -1) / lengths.astype(jnp.float32)[:, None]
    proj_width = partial_proj.shape[1]
    ex_count = lax.axis_size("ex")
    block_width = proj_width // ex_count
    pieces = partial_proj.reshape(examples_dev, ex_count, block_width)
    moved = lax.all_to_all(pieces, "ex", split_axis=1, concat_axis=0, tiled=True)
    summed = lax.psum(moved, "seq")
    owned = summed.astype(jnp.bfloat16).reshape(examples_dev * ex_count, block_width)
    return lax.psum_scatter(
        lax.dot_general(
            owned, query_grads, (((1,), (1,)), ((), ())), preferred_element_type=jnp.float32
        ),
        "ex",
        scatter_dimension=0,
        tiled=True,
    )


def solution(mesh):
    in_specs = (
        P("ex", "seq", None),
        P("ex", "seq", None),
        P("ex"),
        P(),
        P(),
        P(),
        P(),
        P(),
        P(),
        P("seq", "ex"),
    )
    out_specs = P("ex", "seq")
    return jax.shard_map(
        per_device, mesh=mesh, in_specs=in_specs, out_specs=out_specs, check_vma=False
    )
```

profile of v0, /device:TPU:0, one launch (start us, length us, event | category | flops | bytes accessed | tf_op | source)
XLA Modules:
  0.0 92.1 jit_solution(9811729410962465294)
XLA Ops:
  0.0 0.0 copy-start
  0.0 0.9 add_convert_fusion
  0.9 1.2 %convert_multiply_fusion.1 = f32[40,128,64]{1,2,0:T(8,128)S(1)} fusion(bf16[40,128,64]{1,2,0:T(8,128)(2,1)} %param.16, f32[40,128]{1,0:T(8,128)S(1)} %add_convert_fusion), kind=kLoop, calls=%fused_computation.15 | loop fusion | flops 655360 | bytes 1986560 | tf_op jit(solution)/shard_map/mul | solution.py:12
  2.1 2.3 %convolution_convert_fusion = bf16[40,128,64]{1,0,2:T(8,128)(2,1)S(1)} fusion(f32[40,128,64]{1,2,0:T(8,128)S(1)} %convert_multiply_fusion.1, s32[40]{0:T(128)} %param.17), kind=kOutput, calls=%fused_computation.8 | convolution fusion | flops 157615680 | bytes 1966240 | tf_op jit(solution)/shard_map/bc,bik->cik/dot_general | solution.py:13
  4.5 0.2 copy.39
  4.7 0.0 copy-done
  4.7 0.0 copy-start.1
  4.8 1.0 %fusion.18 = bf16[256,128]{0,1:T(8,128)(2,1)S(1)} fusion(bf16[256,5120]{1,0:T(8,128)(2,1)S(1)} %bitcast.46, bf16[1024,64]{0,1:T(8,128)(2,1)S(1)} %bitcast.54, bf16[4096,64]{0,1:T(8,128)(2,1)S(1)} %bitcast.50), kind=kOutput, calls=%fused_computation.18 | convolution fusion | flops 340819968 | bytes 3342336 | tf_op jit(solution)/shard_map/dot_general | solution.py:52
  5.8 0.0 copy-start.3
  5.8 0.1 copy.25
  5.9 0.0 copy-done.1
  5.9 1.8 %convert_multiply_fusion = f32[32,128,128]{2,1,0:T(8,128)S(1)} fusion(bf16[32,128,128]{2,1,0:T(8,128)(2,1)} %param.13, f32[32,128]{1,0:T(8,128)S(1)} %add_convert_fusion.1), kind=kLoop, calls=%fused_computation.6 | loop fusion | flops 1048576 | bytes 3162112 | tf_op jit(solution)/shard_map/mul | solution.py:12
  7.7 0.0 copy-done.3
  7.8 0.0 copy-start.2
  7.8 2.4 %fusion.4 = bf16[32,128,128]{2,0,1:T(8,128)(2,1)S(1)} fusion(f32[32,128,128]{2,1,0:T(8,128)S(1)} %convert_multiply_fusion, s32[32]{0:T(128)S(1)} %copy-done.3), kind=kOutput, calls=%fused_computation.7 | convolution fusion | flops 201851904 | bytes 3145856 | tf_op jit(solution)/shard_map/bc,bik->cik/dot_general | solution.py:13
  10.2 1.4 %copy.21 = bf16[32,128,128]{2,1,0:T(8,128)(2,1)} copy(bf16[32,128,128]{2,0,1:T(8,128)(2,1)S(1)} %fusion.4) | data formatting | bytes 2097152 | tf_op jit(solution)/shard_map/convert_element_type | solution.py:14
  11.6 0.0 copy-done.2
  11.6 0.1 compare_convert_fusion
  11.7 0.0 copy-start.4
  11.7 2.7 %convolution_bitcast_fusion = f32[16,2,8,128]{3,2,1,0:T(8,128)S(1)} fusion(bf16[4096,128]{1,0:T(8,128)(2,1)} %bitcast.47, bf16[256,4096]{1,0:T(8,128)(2,1)} %bitcast.48), kind=kOutput, calls=%fused_computation.16 | convolution fusion | flops 268435456 | bytes 3276800 | tf_op jit(solution)/shard_map/dot_general | solution.py:46
  14.4 0.1 fusion.23
  14.6 0.1 fusion.38
  14.7 0.1 stack.10
  14.8 0.1 stack.9
  14.9 0.7 maximum_divide_fusion
  15.6 4.3 %all-to-all-start = ((f32[2,2,4096]{2,0,1:T(2,128)}), f32[2,2,4096]{2,0,1:T(2,128)S(1)}, u32[]{:S(2)}, u32[]{:S(2)}) async-start(f32[2,2,4096]{2,0,1:T(2,128)} %maximum_divide_fusion), calls=%async_computation | async-start | bytes 131072 | tf_op jit(solution)/shard_map/all_to_all | solution.py:67
  19.9 0.0 copy-done.4
  19.9 0.6 dynamic-slice
  21.1 2.9 %all-to-all-done = f32[2,2,4096]{2,0,1:T(2,128)S(1)} async-done(((f32[2,2,4096]{2,0,1:T(2,128)}), f32[2,2,4096]{2,0,1:T(2,128)S(1)}, u32[]{:S(2)}, u32[]{:S(2)}) %all-to-all-start) | async-done | bytes 65568 | tf_op jit(solution)/shard_map/all_to_all | solution.py:67
  24.0 0.1 all_to_all.16
  24.0 60.9 %psum.7 = bf16[4,1,4096]{2,0,1:T(4,128)(2,1)S(1)} all-reduce(f32[4,1,4096]{2,0,1:T(4,128)S(1)} %all_to_all.16), channel_id=1, replica_groups=mesh['seq'=16,'ex'=2] {'seq'}, use_global_device_ids=true, to_apply=%region_0.0 | all-reduce | flops 16384 | bytes 98304 | tf_op jit(solution)/shard_map/psum | solution.py:68
  85.0 1.6 %fusion.26 = f32[4,128]{1,0:T(4,128)S(1)} fusion(bf16[128,4096]{1,0:T(8,128)(2,1)} %param.19, bf16[4,1,4096]{2,0,1:T(4,128)(2,1)S(1)} %psum.7), kind=kOutput, calls=%fused_computation.27 | convolution fusion | flops 4194304 | bytes 1083392 | tf_op jit(solution)/shard_map/dot_general | solution.py:71
  86.6 4.9 %all-reduce.2 = f32[4,128]{1,0:T(4,128)S(1)} all-reduce(f32[4,128]{1,0:T(4,128)S(1)} %fusion.26), channel_id=2, replica_groups=mesh['seq'=16,'ex'=2] {'ex'}, use_global_device_ids=true, to_apply=%region_1.0.clone | all-reduce | flops 512 | bytes 4096
  91.5 0.6 constant_dynamic-slice_fusion
  (6 shorter events, 0.1 us)
Async XLA Ops:
  0.0 4.7 %copy-start = (bf16[2,128,5120]{2,1,0:T(8,128)(2,1)S(1)}, bf16[2,128,5120]{2,1,0:T(8,128)(2,1)}, u32[]{:S(2)}) copy-start(bf16[2,128,5120]{2,1,0:T(8,128)(2,1)} %param.11) | copy-start | bytes 7864324
  4.7 1.1 %copy-start.1 = (s32[32,128]{1,0:T(8,128)S(1)}, s32[32,128]{1,0:T(8,128)}, u32[]{:S(2)}) copy-start(s32[32,128]{1,0:T(8,128)} %param.15) | copy-start | bytes 49156
  5.8 2.0 %copy-start.3 = (s32[32]{0:T(128)S(1)}, s32[32]{0:T(128)}, u32[]{:S(2)}) copy-start(s32[32]{0:T(128)} %param.14) | copy-start | bytes 388
  7.8 3.9 %copy-start.2 = (s32[2]{0:T(128)S(1)}, s32[2]{0:T(128)}, u32[]{:S(2)}) copy-start(s32[2]{0:T(128)} %param.12) | copy-start | bytes 28
  11.7 8.2 %copy-start.4 = (u32[32]{0:T(128)S(1)}, u32[32]{0:T(128)}, u32[]{:S(2)}) copy-start(u32[32]{0:T(128)} %constant.25) | copy-start | bytes 388
  15.6 8.4 %all-to-all-start = ((f32[2,2,4096]{2,0,1:T(2,128)}), f32[2,2,4096]{2,0,1:T(2,128)S(1)}, u32[]{:S(2)}, u32[]{:S(2)}) async-start(f32[2,2,4096]{2,0,1:T(2,128)} %maximum_divide_fusion), calls=%async_computation | async-start | bytes 131072 | tf_op jit(solution)/shard_map/all_to_all | solution.py:67
where the time goes:
time: 92.4 us; the launch traced here: 92.1 us
  blocking collectives  65.9 us (71%)
  matrix products  10.2 us (11%)
  other arithmetic  4.75 us (5%)
  starting transfers between devices  4.26 us (5%)
  local copies, waits for them, and re-layouts  3.29 us (4%)
  waiting for transfers between devices  2.89 us (3%)
    psum x1, blocking collectives, per_device(): summed = lax.psum(moved, 'seq')  60.9 us
    unnamed x1, blocking collectives  4.93 us
    dot_general x2, matrix products, place(): jnp.einsum('bc,bik->cik', chosen, signed, precision=lax.Precision.HIGHEST)  4.72 us
    all_to_all x1, starting transfers between devices, per_device(): lax.all_to_all(pieces, 'ex', split_axis=1, concat_axis=0, tiled=True)  4.26 us
    mul x2, other arithmetic, place(): sketch_tiles.astype(jnp.float32)  3.08 us
    all_to_all x1, waiting for transfers between devices, per_device(): lax.all_to_all(pieces, 'ex', split_axis=1, concat_axis=0, tiled=True)  2.89 us
    dot_general x1, matrix products, per_device(): jnp.dot(acts.reshape(examples_dev * seq_dev, width), r_in, preferred_elem...  2.74 us
  transfers between devices with their start and end apart: 1, of which 1 were waited for; matrix products, arithmetic and copies ran while one was open for 1% of the time, Pallas kernels for 0%

commit v1 on v0

--- a/solution.py
+++ b/solution.py
@@ -2,6 +2,12 @@
 import jax.numpy as jnp
 from jax import lax
 from jax.sharding import PartitionSpec as P
+
+
+def summed_here(x, name):
+    shards = lax.all_gather(x, name, axis=0, tiled=False)
+    total = shards.sum(axis=0)
+    return total
 
 
 def place(sketch_tiles, block_ids, sign_bits):
@@ -65,7 +71,7 @@
     block_width = proj_width // ex_count
     pieces = partial_proj.reshape(examples_dev, ex_count, block_width)
     moved = lax.all_to_all(pieces, "ex", split_axis=1, concat_axis=0, tiled=True)
-    summed = lax.psum(moved, "seq")
+    summed = summed_here(moved, "seq")
     owned = summed.astype(jnp.bfloat16).reshape(examples_dev * ex_count, block_width)
     return lax.psum_scatter(
         lax.dot_general(

time: 92.4 us -> 84.3 us (0.912)
  blocking collectives: 65.9 us -> 13.1 us
  waiting for transfers between devices: 2.89 us -> 37 us
  between operations: 0.82 us -> 14.2 us
  starting transfers between devices: 4.26 us -> 0.01 us
    psum x1 -> x0, blocking collectives: 60.9 us -> none  [per_device(): summed = lax.psum(moved, 'seq')]
    all_gather x0 -> x1, waiting for transfers between devices: none -> 37 us  [summed_here(): shards = lax.all_gather(x, name, axis=0, tiled=False)]
    all_to_all x0 -> x1, blocking collectives: none -> 8.19 us  [per_device(): lax.all_to_all(pieces, 'ex', split_axis=1, concat_axis=0, tiled=True)]
    all_to_all x1 -> x0, starting transfers between devices: 4.26 us -> none  [per_device(): lax.all_to_all(pieces, 'ex', split_axis=1, concat_axis=0, tiled=True)]
    all_to_all x1 -> x0, waiting for transfers between devices: 2.89 us -> none  [per_device(): lax.all_to_all(pieces, 'ex', split_axis=1, concat_axis=0, tiled=True)]
    reduce_sum x0 -> x1, other arithmetic: none -> 1.39 us  [summed_here(): total = shards.sum(axis=0)]
where the time goes in v1:
time: 84.3 us; the launch traced here: 84 us
  waiting for transfers between devices  37 us (44%)
  between operations  14.2 us (17%)
  blocking collectives  13.1 us (16%)
  matrix products  10.2 us (12%)
  other arithmetic  5.52 us (7%)
  local copies, waits for them, and re-layouts  3.9 us (5%)
    all_gather x1, waiting for transfers between devices, summed_here(): shards = lax.all_gather(x, name, axis=0, tiled=False)  37 us
    all_to_all x1, blocking collectives, per_device(): lax.all_to_all(pieces, 'ex', split_axis=1, concat_axis=0, tiled=True)  8.19 us
    unnamed x1, blocking collectives  4.93 us
    dot_general x2, matrix products, place(): jnp.einsum('bc,bik->cik', chosen, signed, precision=lax.Precision.HIGHEST)  4.72 us
    mul x2, other arithmetic, place(): sketch_tiles.astype(jnp.float32)  3.08 us
    dot_general x1, matrix products, per_device(): jnp.dot(acts.reshape(examples_dev * seq_dev, width), r_in, preferred_elem...  2.75 us
  transfers between devices with their start and end apart: 1, of which 1 were waited for; matrix products, arithmetic and copies ran while one was open for 1% of the time, Pallas kernels for 0%

profile of v1, /device:TPU:0, one launch (start us, length us, event | category | flops | bytes accessed | tf_op | source)
XLA Modules:
  0.0 84.0 jit_solution(12012628926971640523)
XLA Ops:
  6.5 0.0 copy-start
  6.5 0.0 all-gather.2.cloned.1.call-start
  6.5 0.9 %add_convert_fusion = f32[40,128]{1,0:T(8,128)S(1)} fusion(s32[40,128]{1,0:T(8,128)} %param.18), kind=kLoop, calls=%fused_computation.29 | loop fusion | flops 15360 | bytes 40960 | tf_op jit(solution)/shard_map/convert_element_type | solution.py:18
  7.4 1.2 %convert_multiply_fusion.1 = f32[40,128,64]{1,2,0:T(8,128)S(1)} fusion(bf16[40,128,64]{1,2,0:T(8,128)(2,1)} %param.16, f32[40,128]{1,0:T(8,128)S(1)} %add_convert_fusion), kind=kLoop, calls=%fused_computation.15 | loop fusion | flops 655360 | bytes 1986560 | tf_op jit(solution)/shard_map/mul | solution.py:18
  8.7 2.3 %convolution_convert_fusion = bf16[40,128,64]{1,0,2:T(8,128)(2,1)S(1)} fusion(f32[40,128,64]{1,2,0:T(8,128)S(1)} %convert_multiply_fusion.1, s32[40]{0:T(128)} %param.17), kind=kOutput, calls=%fused_computation.8 | convolution fusion | flops 157615680 | bytes 1966240 | tf_op jit(solution)/shard_map/bc,bik->cik/dot_general | solution.py:19
  11.0 0.2 copy.39
  11.3 0.0 copy-done
  11.3 0.0 copy-start.1
  11.3 1.0 %fusion.18 = bf16[256,128]{0,1:T(8,128)(2,1)S(1)} fusion(bf16[256,5120]{1,0:T(8,128)(2,1)S(1)} %bitcast.44, bf16[1024,64]{0,1:T(8,128)(2,1)S(1)} %bitcast.52, bf16[4096,64]{0,1:T(8,128)(2,1)S(1)} %bitcast.48), kind=kOutput, calls=%fused_computation.18 | convolution fusion | flops 340819968 | bytes 3342336 | tf_op jit(solution)/shard_map/dot_general | solution.py:58
  12.3 0.0 copy-start.3
  12.3 0.1 copy.25
  12.4 0.0 copy-done.1
  12.4 1.8 %convert_multiply_fusion = f32[32,128,128]{2,1,0:T(8,128)S(1)} fusion(bf16[32,128,128]{2,1,0:T(8,128)(2,1)} %param.13, f32[32,128]{1,0:T(8,128)S(1)} %add_convert_fusion.1), kind=kLoop, calls=%fused_computation.6 | loop fusion | flops 1048576 | bytes 3162112 | tf_op jit(solution)/shard_map/mul | solution.py:18
  14.3 0.0 copy-done.3
  14.3 0.0 copy-start.2
  14.3 2.4 %fusion.4 = bf16[32,128,128]{2,0,1:T(8,128)(2,1)S(1)} fusion(f32[32,128,128]{2,1,0:T(8,128)S(1)} %convert_multiply_fusion, s32[32]{0:T(128)S(1)} %copy-done.3), kind=kOutput, calls=%fused_computation.7 | convolution fusion | flops 201851904 | bytes 3145856 | tf_op jit(solution)/shard_map/bc,bik->cik/dot_general | solution.py:19
  16.8 1.4 %copy.21 = bf16[32,128,128]{2,1,0:T(8,128)(2,1)} copy(bf16[32,128,128]{2,0,1:T(8,128)(2,1)S(1)} %fusion.4) | data formatting | bytes 2097152 | tf_op jit(solution)/shard_map/convert_element_type | solution.py:20
  18.1 0.0 copy-done.2
  18.1 0.1 compare_convert_fusion
  18.2 0.0 copy-start.4
  18.2 2.7 %convolution_bitcast_fusion = f32[16,2,8,128]{3,2,1,0:T(8,128)S(1)} fusion(bf16[4096,128]{1,0:T(8,128)(2,1)} %bitcast.45, bf16[256,4096]{1,0:T(8,128)(2,1)} %bitcast.46), kind=kOutput, calls=%fused_computation.16 | convolution fusion | flops 268435456 | bytes 3276800 | tf_op jit(solution)/shard_map/dot_general | solution.py:52
  21.0 0.1 fusion.23
  21.1 0.1 fusion.37
  21.2 0.1 stack.10
  21.3 0.1 stack.9
  21.4 0.1 maximum_divide_fusion
  21.5 8.2 %all_to_all.15 = f32[2,2,4096]{2,0,1:T(2,128)S(1)} all-to-all(f32[2,2,4096]{2,0,1:T(2,128)S(1)} %maximum_divide_fusion), channel_id=1, replica_groups=mesh['seq'=16,'ex'=2] {'ex'}, dimensions={1} | all-to-all | bytes 131072 | tf_op jit(solution)/shard_map/all_to_all | solution.py:73
  29.7 0.7 all_gather.6
  30.4 0.0 all-gather.2.cloned.1.call-update
  30.4 0.0 copy-done.4
  30.4 0.6 dynamic-slice
  31.7 37.0 %all-gather.2.cloned.1.call-done = f32[16,4,1,4096]{3,1,2,0:T(4,128)} async-done(((f32[1,4,1,4096]{3,1,2,0:T(4,128)}), f32[16,4,1,4096]{3,1,2,0:T(4,128)}) %all-gather.2.cloned.1.call-update) | async-done | bytes 1048592 | tf_op jit(solution)/shard_map/all_gather | solution.py:8
  68.7 1.4 %reduce_sum.9 = bf16[4,4096]{1,0:T(4,128)(2,1)S(1)} reduce(f32[16,4,1,4096]{3,1,2,0:T(4,128)} %all-gather.2.cloned.1.call-done, f32[]{:T(128)} %constant.20.clone.1), dimensions={0,2}, to_apply=%region_0.0 | reduce | flops 245760 | bytes 1081348 | tf_op jit(solution)/shard_map/reduce_sum | solution.py:9
  70.1 1.6 %fusion.38 = f32[4,128]{1,0:T(4,128)S(1)} fusion(bf16[4,4096]{1,0:T(4,128)(2,1)S(1)} %reduce_sum.9, bf16[128,4096]{1,0:T(8,128)(2,1)} %param.19), kind=kOutput, calls=%fused_computation.44 | convolution fusion | flops 4194304 | bytes 1083392 | tf_op jit(solution)/shard_map/dot_general | solution.py:77
  71.7 4.9 %all-reduce.2 = f32[4,128]{1,0:T(4,128)S(1)} all-reduce(f32[4,128]{1,0:T(4,128)S(1)} %fusion.38), channel_id=2, replica_groups=mesh['seq'=16,'ex'=2] {'ex'}, use_global_device_ids=true, to_apply=%region_1.0.clone | all-reduce | flops 512 | bytes 4096
  76.6 0.6 constant_dynamic-slice_fusion
  (6 shorter events, 0.1 us)
Async XLA Ops:
  6.5 4.7 %copy-start = (bf16[2,128,5120]{2,1,0:T(8,128)(2,1)S(1)}, bf16[2,128,5120]{2,1,0:T(8,128)(2,1)}, u32[]{:S(2)}) copy-start(bf16[2,128,5120]{2,1,0:T(8,128)(2,1)} %param.11) | copy-start | bytes 7864324
  6.5 62.1 %all-gather.2.cloned.1.call-start = ((), (), s32[]{:S(2)}) async-start(), calls=%async_computation.1 | async-start | bytes 1114112 | tf_op jit(solution)/shard_map/all_gather | solution.py:8
  11.3 1.1 %copy-start.1 = (s32[32,128]{1,0:T(8,128)S(1)}, s32[32,128]{1,0:T(8,128)}, u32[]{:S(2)}) copy-start(s32[32,128]{1,0:T(8,128)} %param.15) | copy-start | bytes 49156
  12.3 2.0 %copy-start.3 = (s32[32]{0:T(128)S(1)}, s32[32]{0:T(128)}, u32[]{:S(2)}) copy-start(s32[32]{0:T(128)} %param.14) | copy-start | bytes 388
  14.3 3.8 %copy-start.2 = (s32[2]{0:T(128)S(1)}, s32[2]{0:T(128)}, u32[]{:S(2)}) copy-start(s32[2]{0:T(128)} %param.12) | copy-start | bytes 28
  18.2 12.2 %copy-start.4 = (u32[32]{0:T(128)S(1)}, u32[32]{0:T(128)}, u32[]{:S(2)}) copy-start(u32[32]{0:T(128)} %constant.27) | copy-start | bytes 388
Sparse Core Ops, SparseCore 0:
  30.5 38.1 all-gather.1
